TPU v7x, 32 devices: a whole 2x2x4 slice. The times are simulated.
32 devices in a mesh: groups: 2 (over x), worker: 2 (over core), tensor: 8 (over z, y).
Axes of the slice: x: 2, y: 2, z: 4, core: 2. Of those that a mesh axis runs over, the one named last changes fastest.
Arguments:
- tokens: bfloat16 [1024, 8192], P(('groups', 'worker'), 'tensor'), parts along dimension 0, may hold values from -6 to 6
- norm_gain: float32 [8192], replicated, may hold values from 0.5 to 1.5
- query_weight: bfloat16 [8192, 8192], P(None, 'tensor'), may hold values from -0.0625 to 0.0625
- key_weight: bfloat16 [8192, 1024], P(None, 'tensor'), may hold values from -0.15625 to 0.15625
- value_weight: bfloat16 [8192, 1024], P(None, 'tensor'), may hold values from -0.0625 to 0.0625
- output_weight: bfloat16 [8192, 8192], P('tensor'), may hold values from -0.0625 to 0.0625
- cached_blocks: bfloat16 [8, 1024, 2, 1024], P(('groups', 'worker'), 'tensor'), parts along dimension 0
- cache_length: int32 [8], P('groups'), parts along dimension 0, may hold values from 256 to 1024, as said below
- block_table: int32 [8, 64], P('groups'), parts along dimension 0, may hold values from 0 to 63, each once within a row
- destination: int32 [8], P('groups'), parts along dimension 0, may hold values from 0 to 1, as said below
Outputs:
- attended: bfloat16 [4, 3, 128, 8192], P(('groups', 'worker'), None, None, 'tensor'), parts along dimension 0
There are 2 independent parts, one for each index of `groups`. A program takes and returns all parts, laid end to end along the dimension named above; an argument that names none is the same for every part. Nothing has to cross between parts.
Inputs may be any that keep to these rules, and one draw needn't show every extreme that they name: Exactly 3 sequences have one destination, the others the other; which one is drawn. `cache_length`: some sequence has exactly 1024 cached tokens.
All inputs are finite; a program needn't handle non-finite values.
Results may differ from a plain program's by a relative error of at most 0.02.
The roundings to bfloat16 on the way count: a program that leaves them out, or rounds other values in their place, can miss the bound.
Values may be sent and summed in bfloat16 or wider, within the bound.
No kernel may reach another device: no remote copies, remote signals or barrier semaphores. Data moves between devices by JAX's collectives and lax.ppermute only.
A program may use at most 128 MiB of HBM per device.

v0:
```python
import math

import jax
import jax.numpy as jnp
from jax import lax
from jax.sharding import PartitionSpec as P

D = 8192
KVH = 8
HD = 128
NEW = 128
BLK = 16
CAP = 3


epsilon = 1e-05


def from_partner(block, axis, bit):
    count = lax.axis_size(axis)
    route = []
    for low in range(count):
        high = low | 1 << bit
        if high != low and high < count:
            route += [(low, high), (high, low)]
    return lax.ppermute(block, axis, route)


def rotate(values, positions):
    halfway = HD // 2
    inverse = 500000.0 ** (-(jnp.arange(halfway, dtype=jnp.float32) * 2.0 / HD))
    angles = positions[:, None] * inverse[None, :]
    cosine_table = jnp.concatenate([jnp.cos(angles), jnp.cos(angles)], axis=-1)[:, None, :]
    sine_table = jnp.concatenate([jnp.sin(angles), jnp.sin(angles)], axis=-1)[:, None, :]
    turned = jnp.concatenate([-values[..., halfway:], values[..., :halfway]], axis=-1)
    return values * cosine_table + turned * sine_table


def attend(
    token_rows,
    blocks,
    lengths,
    tables,
    norm_gain,
    query_weight,
    key_weight,
    value_weight,
    output_weight,
):
    tensor_count = lax.axis_size("tensor")
    tensor_index = lax.axis_index("tensor")
    group_width = tensor_count // KVH
    bit_count = group_width.bit_length() - 1
    seq_count = blocks.shape[0]
    total = token_rows.shape[0]
    query_cols = query_weight.shape[1]
    widened = lax.all_gather(token_rows, "tensor", axis=1, tiled=True).astype(jnp.float32)
    scaled = (widened * norm_gain[None, :]).astype(jnp.bfloat16)
    query_sum = jnp.dot(scaled, query_weight, preferred_element_type=jnp.float32)
    key_sum = jnp.dot(scaled, key_weight, preferred_element_type=jnp.float32)
    value_sum = jnp.dot(scaled, value_weight, preferred_element_type=jnp.float32)
    squares = jnp.sum(widened * widened, axis=1)
    factor = lax.rsqrt(squares / D + epsilon)[:, None]
    positions = (
        (lengths[:, None] + jnp.arange(NEW, dtype=jnp.int32)[None, :])
        .reshape(total)
        .astype(jnp.float32)
    )
    heads_here = query_cols // HD
    queries = rotate((query_sum * factor).reshape(total, heads_here, HD), positions).astype(
        jnp.bfloat16
    )
    key_full = (key_sum * factor).astype(jnp.bfloat16)
    value_full = (value_sum * factor).astype(jnp.bfloat16)
    for bit in range(bit_count):
        other_key, other_value = from_partner((key_full, value_full), "tensor", bit)
        upper = tensor_index // (1 << bit) % 2 == 1
        key_full = jnp.where(
            upper,
            jnp.concatenate([other_key, key_full], axis=1),
            jnp.concatenate([key_full, other_key], axis=1),
        )
        value_full = jnp.where(
            upper,
            jnp.concatenate([other_value, value_full], axis=1),
            jnp.concatenate([value_full, other_value], axis=1),
        )
    new_key = rotate(key_full.astype(jnp.float32)[:, None, :], positions)[:, 0, :].astype(
        jnp.bfloat16
    )
    fresh_keys = new_key.reshape(seq_count, NEW, HD)
    fresh_values = value_full.reshape(seq_count, NEW, HD)
    local_tokens = blocks.shape[1]
    inverse_root = 1.0 / math.sqrt(HD)
    query_blocks = queries.reshape(seq_count, NEW, heads_here, HD)
    causal = jnp.arange(NEW)[:, None] >= jnp.arange(NEW)[None, :]
    spread = jnp.repeat(
        blocks.reshape(seq_count, local_tokens, 2, KVH, HD), tensor_count // KVH, axis=3
    )
    arrived = lax.all_to_all(spread, "tensor", split_axis=3, concat_axis=1, tiled=True)
    context = arrived.shape[1]
    old_key = arrived[:, :, 0, 0, :]
    old_value = arrived[:, :, 1, 0, :]
    stored = jnp.arange(context, dtype=jnp.int32)
    logical = jnp.take(tables, stored // BLK, axis=1) * BLK + stored % BLK
    visible = logical < lengths[:, None]
    old_scores = (
        jnp.einsum("sqhd,skd->shqk", query_blocks, old_key, preferred_element_type=jnp.float32)
        * inverse_root
    )
    old_scores = jnp.where(visible[:, None, None, :], old_scores, -1e30)
    new_scores = (
        jnp.einsum("sqhd,skd->shqk", query_blocks, fresh_keys, preferred_element_type=jnp.float32)
        * inverse_root
    )
    new_scores = jnp.where(causal[None, None], new_scores, -1e30)
    largest = jnp.maximum(jnp.max(old_scores, axis=3), jnp.max(new_scores, axis=3))[..., None]
    old_expo = jnp.exp(old_scores - largest)
    new_expo = jnp.exp(new_scores - largest)
    denominator = (jnp.sum(old_expo, axis=3) + jnp.sum(new_expo, axis=3))[..., None]
    old_probs = (old_expo / denominator).astype(jnp.bfloat16)
    new_probs = (new_expo / denominator).astype(jnp.bfloat16)
    mixture = jnp.einsum("shqk,skd->sqhd", old_probs, old_value, preferred_element_type=jnp.float32)
    mixture = mixture + jnp.einsum(
        "shqk,skd->sqhd", new_probs, fresh_values, preferred_element_type=jnp.float32
    )
    attended_rows = mixture.astype(jnp.bfloat16).reshape(total, heads_here * HD)
    partial_value = jnp.dot(attended_rows, output_weight, preferred_element_type=jnp.float32)
    summed = lax.psum_scatter(partial_value, "tensor", scatter_dimension=1, tiled=True)
    return summed.astype(jnp.bfloat16)


def local(
    tokens,
    norm_gain,
    query_weight,
    key_weight,
    value_weight,
    output_weight,
    cached_blocks,
    cache_length,
    block_table,
    destination,
):
    worker_index = lax.axis_index("worker")
    seq_total = destination.shape[0]
    belongs = (destination == worker_index).astype(jnp.int32)
    ranking = jnp.cumsum(belongs) - 1
    matched = (belongs[None, :] == 1) & (
        ranking[None, :] == jnp.arange(CAP, dtype=jnp.int32)[:, None]
    )
    slot_owner = jnp.sum(
        matched.astype(jnp.int32) * jnp.arange(seq_total, dtype=jnp.int32)[None, :], axis=1
    )
    occupied = jnp.any(matched, axis=1)
    local_count = cached_blocks.shape[0]
    owned = worker_index * local_count + jnp.arange(local_count, dtype=jnp.int32)
    mixed = attend(
        tokens,
        cached_blocks,
        jnp.take(cache_length, owned),
        jnp.take(block_table, owned, axis=0),
        norm_gain,
        query_weight,
        key_weight,
        value_weight,
        output_weight,
    )
    everyone = lax.all_gather(mixed, "worker", axis=0, tiled=True)
    placed = jnp.take(everyone.reshape(seq_total, NEW, -1), slot_owner, axis=0)
    result = jnp.where(occupied[:, None, None], placed, jnp.zeros_like(placed))
    return result[None]


def solution(mesh):
    placed = (
        P(("groups", "worker"), "tensor"),
        P(),
        P(None, "tensor"),
        P(None, "tensor"),
        P(None, "tensor"),
        P("tensor", None),
        P(("groups", "worker"), "tensor", None, None),
        P("groups"),
        P("groups", None),
        P("groups"),
    )
    return jax.shard_map(
        local,
        mesh=mesh,
        in_specs=placed,
        out_specs=P(("groups", "worker"), None, None, "tensor"),
        check_vma=False,
    )
```

profile of v0, /device:TPU:13, one launch (start us, length us, event | category | flops | bytes accessed | tf_op | source)
XLA Modules:
  0.0 309.6 jit_solution(4129475814052174620)
XLA Ops:
  6.5 0.7 all-gather.3.cloned.1.call-update
  7.3 2.6 copy.86
  9.8 1.3 copy.87
  11.1 5.7 %all-to-all-start = ((bf16[2,128,2,8,128]{4,1,0,2,3:T(8,128)(2,1)}), bf16[2,128,2,8,128]{4,1,0,2,3:T(8,128)(2,1)S(1)}, u32[]{:S(2)}, u32[]{:S(2)}) async-start(bf16[2,128,2,8,128]{4,1,0,2,3:T(8,128)(2,1)} %copy.87), calls=%async_computation | async-start | bytes 2097152 | tf_op jit(solution)/shard_map/all_to_all | solution.py:100
  16.8 1.3 gather_fusion.2
  18.1 1.2 gather_fusion
  19.5 0.1 copy.80
  19.6 4.0 %gather_fusion.1 = s32[1024,2]{1,0:T(8,128)} fusion(s32[2,64]{0,1:T(8,128)S(1)} %copy.80, s32[1024]{0:T(1024)S(1)} %broadcast_clamp_fusion), kind=kCustom, calls=%fused_computation.1 | custom fusion | bytes 20480 | tf_op jit(solution)/shard_map/jit(_take)/gather | solution.py:105
  23.6 1.2 copy.81
  24.9 0.6 iota_compare_fusion
  25.5 0.1 fusion.68
  25.6 0.5 multiply_cosine_fusion
  26.1 0.1 pad_maximum_fusion
  26.3 0.1 compare_bitcast_fusion
  26.3 0.3 multiply_sine_fusion.1
  26.6 30.2 %all-to-all-done = bf16[2,128,2,8,128]{4,1,0,2,3:T(8,128)(2,1)S(1)} async-done(((bf16[2,128,2,8,128]{4,1,0,2,3:T(8,128)(2,1)}), bf16[2,128,2,8,128]{4,1,0,2,3:T(8,128)(2,1)S(1)}, u32[]{:S(2)}, u32[]{:S(2)}) %all-to-all-start) | async-done | bytes 1048608 | tf_op jit(solution)/shard_map/all_to_all | solution.py:100
  56.8 1.0 copy.88
  57.9 39.9 %all-gather.3.cloned.1.call-done = bf16[256,8192]{1,0:T(8,128)(2,1)} async-done(((bf16[256,1024]{1,0:T(8,128)(2,1)}), bf16[256,8192]{1,0:T(8,128)(2,1)}) %all-gather.3.cloned.1.call-update) | async-done | bytes 4194320 | tf_op jit(solution)/shard_map/all_gather | solution.py:57
  97.8 3.1 %fusion.1 = f32[256]{0:T(256)S(1)} fusion(bf16[256,8192]{1,0:T(8,128)(2,1)} %all-gather.3.cloned.1.call-done), kind=kLoop, calls=%fused_computation.7 | loop fusion | flops 6291200 | bytes 4195328 | tf_op jit(solution)/shard_map/reduce_sum | solution.py:62
  100.9 3.6 %fusion.25 = bf16[256,128]{0,1:T(8,128)(2,1)S(1)} fusion(bf16[8192,128]{1,0:T(8,128)(2,1)S(1)} %copy-done, bf16[256,8192]{1,0:T(8,128)(2,1)} %all-gather.3.cloned.1.call-done, f32[8192]{0:T(1024)} %param.11, f32[256]{0:T(256)S(1)} %add_rsqrt_fusion), kind=kOutput, calls=%fused_computation.28 | convolution fusion | flops 543227904 | bytes 6390784 | tf_op jit(solution)/shard_map/dot_general | solution.py:61
  104.5 0.6 reshape.302
  105.2 4.3 %fusion.31 = f32[256,128]{0,1:T(8,128)S(1)} fusion(bf16[8192,128]{1,0:T(8,128)(2,1)} %param.13, bf16[256,8192]{1,0:T(8,128)(2,1)} %all-gather.3.cloned.1.call-done, f32[8192]{0:T(1024)S(1)} %copy-done.6, f32[256]{0:T(256)S(1)} %add_rsqrt_fusion), kind=kOutput, calls=%fused_computation.30 | convolution fusion | flops 543260672 | bytes 6456320 | tf_op jit(solution)/shard_map/dot_general | solution.py:60
  109.6 0.1 copy.106
  109.7 9.5 %fusion.11 = f32[256,1024]{1,0:T(8,128)S(1)} fusion(bf16[8192,1024]{1,0:T(8,128)(2,1)} %param.12, bf16[256,8192]{1,0:T(8,128)(2,1)} %all-gather.3.cloned.1.call-done, f32[8192]{0:T(1024)} %param.11, f32[256]{0:T(256)S(1)} %add_rsqrt_fusion), kind=kOutput, calls=%fused_computation.18 | convolution fusion | flops 4301520896 | bytes 22053888 | tf_op jit(solution)/shard_map/dot_general | solution.py:59
  119.2 0.3 copy.109
  119.6 0.2 copy.110
  119.8 0.9 slice_negate_fusion
  120.7 0.4 copy.104
  121.1 1.5 copy.105
  122.6 0.4 fusion.35
  122.9 0.3 fusion.69
  123.3 2.6 bitcast_reduce_fusion
  125.9 0.2 fusion.36
  126.1 2.1 fusion.3
  128.3 2.5 fusion.17
  130.7 0.4 fusion.18
  131.1 0.3 copy.96
  131.5 0.1 slice-done.2
  131.6 1.2 slice-done.3
  132.8 6.7 %fusion.38 = f32[256,8192]{1,0:T(8,128)} fusion(bf16[1024,8192]{1,0:T(8,128)(2,1)S(1)} %bitcast.101, bf16[32,8,8,128]{3,2,1,0:T(8,128)(2,1)S(1)} %bitcast.109), kind=kOutput, calls=%fused_computation.40 | convolution fusion | flops 4294967296 | bytes 25690112 | tf_op jit(solution)/shard_map/dot_general | solution.py:128
  139.6 148.0 %reduce-scatter.2.cloned.1.call-done = f32[256,1024]{1,0:T(8,128)} async-done(((f32[256,8192]{1,0:T(8,128)}), f32[256,1024]{1,0:T(8,128)}) %reduce-scatter.2.cloned.1.call-update) | async-done | bytes 1048592 | tf_op jit(solution)/shard_map/reduce_scatter | solution.py:129
  287.6 2.1 convert_element_type.67
  289.8 0.2 reduce-window.8
  290.0 0.1 select_reduce_fusion
  290.1 0.1 fusion.61
  290.2 10.0 %all-gather.5.cloned.1.call-done = bf16[512,1024]{1,0:T(8,128)(2,1)} async-done(((bf16[256,1024]{1,0:T(8,128)(2,1)}), bf16[512,1024]{1,0:T(8,128)(2,1)}) %all-gather.5.cloned.1.call-update) | async-done | bytes 1048592 | tf_op jit(solution)/shard_map/all_gather | solution.py:169
  300.2 1.8 gather_fusion.3
  302.0 1.0 fusion.37
  (46 shorter events, 0.4 us)
Async XLA Ops:
  6.5 94.4 %copy-start = (bf16[8192,128]{1,0:T(8,128)(2,1)S(1)}, bf16[8192,128]{1,0:T(8,128)(2,1)}, u32[]{:S(2)}) copy-start(bf16[8192,128]{1,0:T(8,128)(2,1)} %param.14) | copy-start | bytes 6291460
  6.5 91.3 %all-gather.3.cloned.1.call-start = ((), (), s32[]{:S(2)}) async-start(), calls=%async_computation.2 | async-start | bytes 4718592 | tf_op jit(solution)/shard_map/all_gather | solution.py:57
  11.1 45.7 %all-to-all-start = ((bf16[2,128,2,8,128]{4,1,0,2,3:T(8,128)(2,1)}), bf16[2,128,2,8,128]{4,1,0,2,3:T(8,128)(2,1)S(1)}, u32[]{:S(2)}, u32[]{:S(2)}) async-start(bf16[2,128,2,8,128]{4,1,0,2,3:T(8,128)(2,1)} %copy.87), calls=%async_computation | async-start | bytes 2097152 | tf_op jit(solution)/shard_map/all_to_all | solution.py:100
  16.8 270.8 %reduce-scatter.2.cloned.1.call-start = ((), (), s32[]{:S(2)}) async-start(), calls=%async_computation.3 | async-start | bytes 9437184 | tf_op jit(solution)/shard_map/reduce_scatter | solution.py:129
  57.9 47.3 %copy-start.6 = (f32[8192]{0:T(1024)S(1)}, f32[8192]{0:T(1024)}, u32[]{:S(2)}) copy-start(f32[8192]{0:T(1024)} %param.11) | copy-start | bytes 98308
  119.2 3.7 %copy-start.3 = (pred[128,128]{0,1:T(8,128)(4,1)S(1)}, pred[128,128]{0,1:T(8,128)(4,1)}, u32[]{:S(2)}) copy-start(pred[128,128]{0,1:T(8,128)(4,1)} %iota_compare_fusion) | copy-start | bytes 49156
  123.3 4.9 %copy-start.2 = (bf16[2,8,128,2,1,128]{5,2,1,0,3,4:T(8,128)(2,1)S(1)}, bf16[2,8,128,2,1,128]{5,2,1,0,3,4:T(8,128)(2,1)}, u32[]{:S(2)}) copy-start(bf16[2,8,128,2,1,128]{5,2,1,0,3,4:T(8,128)(2,1)} %copy.88) | copy-start | bytes 3145732
  126.1 5.4 %slice-start = ((s8[16777216]{0:T(1024)(128)(4,1)}), s8[4194304]{0:T(1024)(128)(4,1)S(1)}, s32[]{:S(2)}) async-start(s8[16777216]{0:T(1024)(128)(4,1)} %bitcast.100), calls=%async_computation.5 | async-start | bytes 8388608
  128.2 2.5 copy-start.4
  128.2 3.3 %slice-start.1 = ((s8[16777216]{0:T(1024)(128)(4,1)}), s8[4194304]{0:T(1024)(128)(4,1)S(1)}, s32[]{:S(2)}) async-start(s8[16777216]{0:T(1024)(128)(4,1)} %bitcast.100), calls=%async_computation.6 | async-start | bytes 8388608
  128.2 3.4 %slice-start.2 = ((s8[16777216]{0:T(1024)(128)(4,1)}), s8[4194304]{0:T(1024)(128)(4,1)S(1)}, s32[]{:S(2)}) async-start(s8[16777216]{0:T(1024)(128)(4,1)} %bitcast.100), calls=%async_computation.7 | async-start | bytes 8388608
  128.3 4.6 %slice-start.3 = ((s8[16777216]{0:T(1024)(128)(4,1)}), s8[4194304]{0:T(1024)(128)(4,1)S(1)}, s32[]{:S(2)}) async-start(s8[16777216]{0:T(1024)(128)(4,1)} %bitcast.100), calls=%async_computation.8 | async-start | bytes 8388608
  132.8 170.2 %copy-start.1 = (bf16[8192,128]{1,0:T(8,128)(2,1)S(1)}, bf16[8192,128]{1,0:T(8,128)(2,1)}, u32[]{:S(2)}) copy-start(bf16[8192,128]{1,0:T(8,128)(2,1)} %param.14) | copy-start | bytes 6291460
  139.6 150.2 %copy-start.5 = (s32[4]{0:T(128)S(1)}, s32[4]{0:T(128)}, u32[]{:S(2)}) copy-start(s32[4]{0:T(128)} %param.19) | copy-start | bytes 52
  139.6 160.6 %all-gather.5.cloned.1.call-start = ((), (), s32[]{:S(2)}) async-start(), calls=%async_computation.4 | async-start | bytes 1572864 | tf_op jit(solution)/shard_map/all_gather | solution.py:169
Sparse Core Ops, SparseCore 0:
  9.5 88.2 all-gather.2
  139.7 147.8 reduce-scatter.1
  289.9 10.2 all-gather.4
where the time goes:
time: 311 us; the launch traced here: 310 us
  waiting for transfers between devices  229 us (74%)
  matrix products  30 us (10%)
  local copies, waits for them, and re-layouts  19.5 us (6%)
  between operations  13.4 us (4%)
  other arithmetic  12.2 us (4%)
  starting transfers between devices  5.71 us (2%)
    reduce_scatter x1, waiting for transfers between devices, attend(): lax.psum_scatter(partial_value, 'tensor', scatter_dimension=1, tiled=True)  148 us
    all_gather x1, waiting for transfers between devices, attend(): lax.all_gather(token_rows, 'tensor', axis=1, tiled=True).astype(jnp.float32)  39.9 us
    all_to_all x1, waiting for transfers between devices, attend(): lax.all_to_all(spread, 'tensor', split_axis=3, concat_axis=1, tiled=True)  30.2 us
    all_gather x1, waiting for transfers between devices, local(): everyone = lax.all_gather(mixed, 'worker', axis=0, tiled=True)  9.97 us
    dot_general x1, matrix products, attend(): jnp.dot(scaled, query_weight, preferred_element_type=jnp.float32)  9.52 us
    dot_general x1, matrix products, attend(): jnp.dot(attended_rows, output_weight, preferred_element_type=jnp.float32)  6.74 us
  transfers between devices with their start and end apart: 4, of which 4 were waited for; matrix products, arithmetic and copies ran while one was open for 5% of the time, Pallas kernels for 0%

commit v1 on v0

--- a/solution.py
+++ b/solution.py
@@ -3,6 +3,8 @@
 import jax
 import jax.numpy as jnp
 from jax import lax
+from jax.experimental import pallas as pl
+from jax.experimental.pallas import tpu as pltpu
 from jax.sharding import PartitionSpec as P
 
 D = 8192
@@ -14,6 +16,300 @@
 
 
 epsilon = 1e-05
+hidden = -1e30
+wide = jnp.float32
+narrow = jnp.bfloat16
+
+
+def tables_of(positions):
+    halfway = HD // 2
+    inverse = 500000.0 ** (-(jnp.arange(halfway, dtype=wide) * 2.0 / HD))
+    angles = positions[..., None] * inverse
+    cosine, sine = jnp.cos(angles), jnp.sin(angles)
+    return (
+        jnp.concatenate([cosine, cosine], axis=-1),
+        jnp.concatenate([-sine, sine], axis=-1),
+    )
+
+
+class Plane:
+    def __init__(self, count):
+        self.count = count
+        self.near = [(i, i ^ 1) for i in range(count)]
+        self.pair = [(i, i ^ 2) for i in range(count)]
+        middle = [(2, 4), (3, 5)]
+        edge = [(2, 0), (3, 1), (4, 6), (5, 7)]
+        self.middle = middle + [(b, a) for a, b in middle]
+        self.outward = edge
+        self.inward = [(b, a) for a, b in edge]
+        far = lax.axis_index("tensor") // 2
+        self.central = (far == 1) | (far == 2)
+
+    def send(self, block, route):
+        return lax.ppermute(block, "tensor", route)
+
+    def gather(self, own):
+        from_pair = self.send(own, self.pair)
+        across = self.send(own, self.middle)
+        near_own = self.send(own, self.near)
+        across_pair = self.send(from_pair, self.middle)
+        near_pair = self.send(from_pair, self.near)
+        relayed = self.send(across, self.outward)
+        third = jnp.where(self.central, across, relayed)
+        near_third = self.send(third, self.near)
+        relayed_pair = self.send(across_pair, self.outward)
+        fourth = jnp.where(self.central, across_pair, relayed_pair)
+        near_fourth = self.send(fourth, self.near)
+        return [own, near_own, from_pair, near_pair, third, near_third, fourth, near_fourth]
+
+    def offsets(self):
+        six = jnp.where(self.central, 6, 4)
+        four = jnp.where(self.central, 4, 6)
+        return jnp.stack([jnp.int32(v) for v in (0, 1, 2, 3)] + [six, six ^ 1, four, four ^ 1])
+
+    def scatter(self, blocks):
+        part = {}
+        for far in (3, 2, 1, 0):
+            other = self.send(blocks[2 * far + 1], self.near)
+            part[far] = blocks[2 * far].astype(wide) + other.astype(wide)
+        inbound_far = self.send(part[3].astype(narrow), self.inward)
+        inbound_two = self.send(part[2].astype(narrow), self.inward)
+        to_pair = (part[2] + inbound_far.astype(wide)).astype(narrow)
+        crossed_pair = self.send(to_pair, self.middle)
+        to_cross = (part[3] + inbound_two.astype(wide)).astype(narrow)
+        crossed = self.send(to_cross, self.middle)
+        last = (part[1] + crossed_pair.astype(wide)).astype(narrow)
+        from_pair = self.send(last, self.pair)
+        return (part[0] + from_pair.astype(wide) + crossed.astype(wide)).astype(narrow)
+
+    def exchange(self, pieces):
+        index = lax.axis_index("tensor")
+        rest = pieces.shape[1:]
+        grid = pieces.reshape((self.count // 2, 2) + rest)
+        keep = lax.dynamic_index_in_dim(grid, index % 2, 1, keepdims=False)
+        give = lax.dynamic_index_in_dim(grid, 1 - index % 2, 1, keepdims=False)
+        taken = self.send(give, self.near)
+        arrived = []
+        for far in range(self.count // 2):
+            target = index // 2 ^ far
+            block = jnp.stack(
+                [
+                    lax.dynamic_index_in_dim(keep, target, 0, keepdims=False),
+                    lax.dynamic_index_in_dim(taken, target, 0, keepdims=False),
+                ]
+            )
+            if far:
+                block = self.send(block, [(i, i ^ 2 * far) for i in range(self.count)])
+            arrived.append(block)
+        return arrived
+
+
+def project(chunks, sources, gain, query_weight, key_weight, value_weight, cosine, sine):
+    count = len(chunks)
+    rows, width = chunks[0].shape
+    query_cols = query_weight.shape[1]
+    key_cols = key_weight.shape[1]
+    heads = query_cols // HD
+
+    def body(source_ref, *refs):
+        chunk_refs = refs[:count]
+        gain_ref, query_hbm, key_hbm, value_hbm, cosine_ref, sine_ref = refs[count : count + 6]
+        query_out, key_out, value_out = refs[count + 6 : count + 9]
+        query_buf, key_buf, value_buf, query_acc, key_acc, value_acc, sems = refs[count + 9 :]
+        copies = []
+        for step in range(count):
+            start = source_ref[step] * width
+            group = [
+                pltpu.make_async_copy(hbm.at[pl.ds(start, width), :], buf.at[step], sems.at[k, step])
+                for k, (hbm, buf) in enumerate(
+                    ((query_hbm, query_buf), (key_hbm, key_buf), (value_hbm, value_buf))
+                )
+            ]
+            for copy in group:
+                copy.start()
+            copies.append(group)
+        squares = jnp.zeros((rows, 1), wide)
+        for step in range(count):
+            values = chunk_refs[step][...].astype(wide)
+            squares = squares + jnp.sum(values * values, axis=1, keepdims=True)
+            scaled = (values * gain_ref[source_ref[step]]).astype(narrow)
+            for copy in copies[step]:
+                copy.wait()
+            for acc, buf in ((query_acc, query_buf), (key_acc, key_buf), (value_acc, value_buf)):
+                product = jnp.dot(scaled, buf[step], preferred_element_type=wide)
+                if step:
+                    acc[...] += product
+                else:
+                    acc[...] = product
+        factor = lax.rsqrt(squares / D + epsilon)
+        cosines, sines = cosine_ref[...], sine_ref[...]
+        for head in range(heads):
+            raw = query_acc[:, head * HD : (head + 1) * HD] * factor
+            turned = pltpu.roll(raw, HD // 2, axis=1)
+            query_out[head] = (raw * cosines + turned * sines).astype(narrow)
+        key_out[...] = (key_acc[...] * factor).astype(narrow)
+        value_out[...] = (value_acc[...] * factor).astype(narrow)
+
+    vmem = pl.BlockSpec(memory_space=pltpu.VMEM)
+    hbm = pl.BlockSpec(memory_space=pl.ANY)
+    return pl.pallas_call(
+        body,
+        out_shape=(
+            jax.ShapeDtypeStruct((heads, rows, HD), narrow),
+            jax.ShapeDtypeStruct((rows, key_cols), narrow),
+            jax.ShapeDtypeStruct((rows, key_cols), narrow),
+        ),
+        in_specs=[pl.BlockSpec(memory_space=pltpu.SMEM)]
+        + [vmem] * count
+        + [vmem, hbm, hbm, hbm, vmem, vmem],
+        out_specs=(vmem, vmem, vmem),
+        scratch_shapes=[
+            pltpu.VMEM((count, width, query_cols), narrow),
+            pltpu.VMEM((count, width, key_cols), narrow),
+            pltpu.VMEM((count, width, key_cols), narrow),
+            pltpu.VMEM((rows, query_cols), wide),
+            pltpu.VMEM((rows, key_cols), wide),
+            pltpu.VMEM((rows, key_cols), wide),
+            pltpu.SemaphoreType.DMA((3, count)),
+        ],
+        name="project",
+    )(sources, *chunks, gain, query_weight, key_weight, value_weight, cosine, sine)
+
+
+def attend_and_mix(index, sequence, query, key_raw, value, cosine, sine, visible, stored, weight):
+    heads, rows, _ = query.shape
+    fars = len(stored)
+    local_tokens = stored[0].shape[3]
+    devices = 2 * fars
+    context = devices * local_tokens
+    cols = weight.shape[1] // devices
+    inner = weight.shape[0]
+    root = 1.0 / math.sqrt(HD)
+
+    def body(index_ref, query_ref, key_ref, value_ref, cosine_ref, sine_ref, visible_ref, *refs):
+        stored_refs = refs[:fars]
+        weight_hbm = refs[fars]
+        outs = refs[fars + 1 : fars + 1 + devices]
+        weight_buf, keys, values, mixed, staged, sems, out_sems = refs[fars + 1 + devices :]
+        here = index_ref[0]
+        order = [2 * far + near for far in reversed(range(fars)) for near in (1, 0)]
+        loads = {}
+        for slot in order:
+            loads[slot] = pltpu.make_async_copy(
+                weight_hbm.at[:, pl.ds((here ^ slot) * cols, cols)], weight_buf.at[slot], sems.at[slot]
+            )
+            loads[slot].start()
+        for far in range(fars):
+            for near in (0, 1):
+                start = (here ^ (2 * far + near)) * local_tokens
+                keys[pl.ds(start, local_tokens), :] = stored_refs[far][near, 0, 0]
+                values[pl.ds(start, local_tokens), :] = stored_refs[far][near, 0, 1]
+        raw = key_ref[...].astype(wide)
+        turned = pltpu.roll(raw, HD // 2, axis=1)
+        new_key = (raw * cosine_ref[...] + turned * sine_ref[...]).astype(narrow)
+        new_value = value_ref[...]
+        seen = visible_ref[...] > 0
+        causal = lax.broadcasted_iota(jnp.int32, (rows, rows), 0) >= lax.broadcasted_iota(
+            jnp.int32, (rows, rows), 1
+        )
+        across = (((1,), (1,)), ((), ()))
+        for head in range(heads):
+            own = query_ref[head]
+            old = lax.dot_general(own, keys[...], across, preferred_element_type=wide) * root
+            old = jnp.where(seen, old, hidden)
+            new = lax.dot_general(own, new_key, across, preferred_element_type=wide) * root
+            new = jnp.where(causal, new, hidden)
+            largest = jnp.maximum(
+                jnp.max(old, axis=1, keepdims=True), jnp.max(new, axis=1, keepdims=True)
+            )
+            old = jnp.exp(old - largest)
+            new = jnp.exp(new - largest)
+            total = jnp.sum(old, axis=1, keepdims=True) + jnp.sum(new, axis=1, keepdims=True)
+            share = 1.0 / total
+            mix = jnp.dot((old * share).astype(narrow), values[...], preferred_element_type=wide)
+            mix = mix + jnp.dot((new * share).astype(narrow), new_value, preferred_element_type=wide)
+            mixed[:, head * HD : (head + 1) * HD] = mix.astype(narrow)
+        stores = []
+        for slot in order:
+            loads[slot].wait()
+            product = jnp.dot(mixed[...], weight_buf[slot], preferred_element_type=wide)
+            staged[slot] = product.astype(narrow)
+            store = pltpu.make_async_copy(staged.at[slot], outs[slot], out_sems.at[slot])
+            store.start()
+            stores.append(store)
+        for store in stores:
+            store.wait()
+
+    vmem = pl.BlockSpec(memory_space=pltpu.VMEM)
+    hbm = pl.BlockSpec(memory_space=pl.ANY)
+    piece = pl.BlockSpec((2, 1, 2, local_tokens, HD), lambda i: (0, sequence, 0, 0, 0))
+
+    def whole(array):
+        return pl.BlockSpec(array.shape, lambda i, n=array.ndim: (0,) * n)
+
+    return pl.pallas_call(
+        body,
+        grid=(1,),
+        out_shape=[jax.ShapeDtypeStruct((rows, cols), narrow)] * devices,
+        in_specs=[pl.BlockSpec(memory_space=pltpu.SMEM)]
+        + [whole(a) for a in (query, key_raw, value, cosine, sine, visible)]
+        + [piece] * fars
+        + [hbm],
+        out_specs=[hbm] * devices,
+        scratch_shapes=[
+            pltpu.VMEM((devices, inner, cols), narrow),
+            pltpu.VMEM((context, HD), narrow),
+            pltpu.VMEM((context, HD), narrow),
+            pltpu.VMEM((rows, inner), narrow),
+            pltpu.VMEM((devices, rows, cols), narrow),
+            pltpu.SemaphoreType.DMA((devices,)),
+            pltpu.SemaphoreType.DMA((devices,)),
+        ],
+        name="attend_and_mix",
+    )(index, query, key_raw, value, cosine, sine, visible, *stored, weight)
+
+
+def attend_on_plane(
+    token_rows,
+    blocks,
+    lengths,
+    tables,
+    norm_gain,
+    query_weight,
+    key_weight,
+    value_weight,
+    output_weight,
+):
+    count = lax.axis_size("tensor")
+    index = lax.axis_index("tensor")
+    plane = Plane(count)
+    seq_count, local_tokens = blocks.shape[0], blocks.shape[1]
+    width = token_rows.shape[1]
+    logical = tables[:, :, None] * BLK + jnp.arange(BLK, dtype=jnp.int32)
+    logical = logical.reshape(seq_count, 1, -1)
+    visible = (logical < lengths[:, None, None]).astype(wide)
+    positions = (lengths[:, None] + jnp.arange(NEW, dtype=jnp.int32)[None, :]).astype(wide)
+    cosine, sine = tables_of(positions)
+    gain = norm_gain.reshape(count, 1, width)
+    sources = index ^ plane.offsets()
+    pieces = blocks.reshape(seq_count, local_tokens, 2, count, HD).transpose(3, 0, 2, 1, 4)
+    rows = token_rows.reshape(seq_count, NEW, width)
+    chunks = [plane.gather(rows[s]) for s in range(seq_count)]
+    stored = plane.exchange(pieces)
+    results = []
+    for s in range(seq_count):
+        query, key_raw, value = project(
+            chunks[s], sources, gain, query_weight, key_weight, value_weight, cosine[s], sine[s]
+        )
+        partial = attend_and_mix(
+            index[None], s, query, key_raw, value, cosine[s], sine[s], visible[s], stored, output_weight
+        )
+        results.append(plane.scatter(partial))
+    return results
+
+
+def fits_plane(count):
+    return count == KVH and count == 2 * 4
 
 
 def from_partner(block, axis, bit):
@@ -36,7 +332,7 @@
     return values * cosine_table + turned * sine_table
 
 
-def attend(
+def attend_anywhere(
     token_rows,
     blocks,
     lengths,
@@ -101,8 +397,7 @@
     context = arrived.shape[1]
     old_key = arrived[:, :, 0, 0, :]
     old_value = arrived[:, :, 1, 0, :]
-    stored = jnp.arange(context, dtype=jnp.int32)
-    logical = jnp.take(tables, stored // BLK, axis=1) * BLK + stored % BLK
+    logical = (tables[:, :, None] * BLK + jnp.arange(BLK, dtype=jnp.int32)).reshape(seq_count, context)
     visible = logical < lengths[:, None]
     old_scores = (
         jnp.einsum("sqhd,skd->shqk", query_blocks, old_key, preferred_element_type=jnp.float32)
@@ -127,7 +422,8 @@
     attended_rows = mixture.astype(jnp.bfloat16).reshape(total, heads_here * HD)
     partial_value = jnp.dot(attended_rows, output_weight, preferred_element_type=jnp.float32)
     summed = lax.psum_scatter(partial_value, "tensor", scatter_dimension=1, tiled=True)
-    return summed.astype(jnp.bfloat16)
+    finished = summed.astype(jnp.bfloat16).reshape(seq_count, NEW, -1)
+    return [finished[s] for s in range(seq_count)]
 
 
 def local(
@@ -143,33 +439,37 @@
     destination,
 ):
     worker_index = lax.axis_index("worker")
+    worker_count = lax.axis_size("worker")
     seq_total = destination.shape[0]
     belongs = (destination == worker_index).astype(jnp.int32)
-    ranking = jnp.cumsum(belongs) - 1
+    ranking = jnp.sum(jnp.tril(jnp.broadcast_to(belongs, (seq_total, seq_total))), axis=1) - 1
     matched = (belongs[None, :] == 1) & (
         ranking[None, :] == jnp.arange(CAP, dtype=jnp.int32)[:, None]
     )
-    slot_owner = jnp.sum(
-        matched.astype(jnp.int32) * jnp.arange(seq_total, dtype=jnp.int32)[None, :], axis=1
-    )
-    occupied = jnp.any(matched, axis=1)
     local_count = cached_blocks.shape[0]
-    owned = worker_index * local_count + jnp.arange(local_count, dtype=jnp.int32)
-    mixed = attend(
+    first = worker_index * local_count
+    run = attend_on_plane if fits_plane(lax.axis_size("tensor")) else attend_anywhere
+    own = run(
         tokens,
         cached_blocks,
-        jnp.take(cache_length, owned),
-        jnp.take(block_table, owned, axis=0),
+        lax.dynamic_slice_in_dim(cache_length, first, local_count, 0),
+        lax.dynamic_slice_in_dim(block_table, first, local_count, 0),
         norm_gain,
         query_weight,
         key_weight,
         value_weight,
         output_weight,
     )
-    everyone = lax.all_gather(mixed, "worker", axis=0, tiled=True)
-    placed = jnp.take(everyone.reshape(seq_total, NEW, -1), slot_owner, axis=0)
-    result = jnp.where(occupied[:, None, None], placed, jnp.zeros_like(placed))
-    return result[None]
+    slots = [jnp.zeros_like(own[0]) for _ in range(CAP)]
+    for shift in range(worker_count):
+        route = [(w, (w + shift) % worker_count) for w in range(worker_count)]
+        start = (worker_index - shift) % worker_count * local_count
+        taken = lax.dynamic_slice_in_dim(matched, start, local_count, 1)
+        for s in range(local_count):
+            block = lax.ppermute(own[s], "worker", route) if shift else own[s]
+            for k in range(CAP):
+                slots[k] = jnp.where(taken[k, s], block, slots[k])
+    return jnp.stack(slots)[None]
 
 
 def solution(mesh):

time: 311 us -> 173 us (0.56)
  waiting for transfers between devices: 229 us -> 22.8 us
  starting transfers between devices: 5.71 us -> 79 us
  Pallas kernels: 0 us -> 39.9 us
  matrix products: 30 us -> 0 us
  between operations: 13.4 us -> 0.75 us
  local copies, waits for them, and re-layouts: 19.5 us -> 7.91 us
  other arithmetic: 12.2 us -> 21.1 us
    reduce_scatter x1 -> x0, waiting for transfers between devices: 148 us -> none  [attend(): lax.psum_scatter(partial_value, 'tensor', scatter_dimension=1, tiled=True)]
    ppermute x0 -> x42, starting transfers between devices: none -> 79 us  [the longest x40 56 us: send(): return lax.ppermute(block, 'tensor', route)]
    all_gather x2 -> x0, waiting for transfers between devices: 49.9 us -> none  [the longest x1 39.9 us: attend(): lax.all_gather(token_rows, 'tensor', axis=1, tiled=True).astype(jnp.float32)]
    pallas_call x0 -> x4, Pallas kernels: none -> 39.9 us  [the longest x2 20 us: project(): pl.pallas_call(body, out_shape=(jax.ShapeDtypeStruct((heads, rows, HD), n...]
    all_to_all x1 -> x0, waiting for transfers between devices: 30.2 us -> none  [attend(): lax.all_to_all(spread, 'tensor', split_axis=3, concat_axis=1, tiled=True)]
    dot_general x8 -> x0, matrix products: 30 us -> none  [the longest x1 9.52 us: attend(): jnp.dot(scaled, query_weight, preferred_element_type=jnp.float32)]
    ppermute x0 -> x42, waiting for transfers between devices: none -> 22.8 us  [the longest x40 22.4 us: send(): return lax.ppermute(block, 'tensor', route)]
    gather x5 -> x0, local copies, waits for them, and re-layouts: 9.62 us -> none  [the longest x2 5.26 us: attend(): logical = jnp.take(tables, stored // BLK, axis=1) * BLK + stored % BLK]
  transfers between devices with their start and end apart: 4 -> 42, of which waited for: 4 -> 12; matrix products, arithmetic and copies ran while one was open for 5% -> 10% of each run, Pallas kernels for 0% -> 23%
where the time goes in v1:
time: 173 us; the launch traced here: 172 us
  starting transfers between devices  79 us (46%)
  Pallas kernels  39.9 us (23%)
  waiting for transfers between devices  22.8 us (13%)
  other arithmetic  21.1 us (12%)
  local copies, waits for them, and re-layouts  7.91 us (5%)
    ppermute x40, starting transfers between devices, send(): return lax.ppermute(block, 'tensor', route)  56 us
    ppermute x2, starting transfers between devices, local(): block = lax.ppermute(own[s], 'worker', route) if shift else own[s]  23.1 us
    ppermute x40, waiting for transfers between devices, send(): return lax.ppermute(block, 'tensor', route)  22.4 us
    pallas_call x2, Pallas kernels, project(): pl.pallas_call(body, out_shape=(jax.ShapeDtypeStruct((heads, rows, HD), n...  20 us
    pallas_call x2, Pallas kernels, attend_and_mix(): pl.pallas_call(body, grid=(1,), out_shape=[jax.ShapeDtypeStruct((rows, co...  19.9 us
    another operation x1, other arithmetic, local(): return jnp.stack(slots)[None]  7.69 us
  transfers between devices with their start and end apart: 42, of which 12 were waited for; matrix products, arithmetic and copies ran while one was open for 10% of the time, Pallas kernels for 23%

profile of v1, /device:TPU:13, one launch (start us, length us, event | category | flops | bytes accessed | tf_op | source)
XLA Modules:
  0.0 171.6 jit_solution(15509571705943271919)
XLA Ops:
  0.0 1.1 fusion.13
  1.3 4.3 %collective-permute-start.26 = (bf16[128,1024]{1,0:T(8,128)(2,1)S(1)}, bf16[128,1024]{1,0:T(8,128)(2,1)}, u32[]{:S(2)}, u32[]{:S(2)}) collective-permute-start(bf16[128,1024]{1,0:T(8,128)(2,1)S(1)} %get-tuple-element.60.refs_0_), channel_id=1, source_target_pairs={{2,4},{3,5},{4,2},{5,3},{10,12},{11,13},{12,10},{13,11},{18,20},{1... | collective-permute-start | bytes 786440 | tf_op jit(solution)/shard_map/ppermute | solution.py:49
  5.7 1.9 %collective-permute-start.3 = (bf16[128,1024]{1,0:T(8,128)(2,1)S(1)}, bf16[128,1024]{1,0:T(8,128)(2,1)}, u32[]{:S(2)}, u32[]{:S(2)}) collective-permute-start(bf16[128,1024]{1,0:T(8,128)(2,1)S(1)} %get-tuple-element.61.refs_0_), channel_id=1, source_target_pairs={{2,4},{3,5},{4,2},{5,3},{10,12},{11,13},{12,10},{13,11},{18,20},{1... | collective-permute-start | bytes 786440 | tf_op jit(solution)/shard_map/ppermute | solution.py:49
  7.7 1.7 %reshape.124 = bf16[2,128,2,8,128]{4,3,2,1,0:T(8,128)(2,1)S(1)} reshape(bf16[2,128,2,1024]{3,2,1,0:T(2,128)(2,1)} %param.16) | data formatting | bytes 2097152 | tf_op jit(solution)/shard_map/reshape | solution.py:295
  13.9 2.8 %collective-permute-start.27 = (bf16[128,1024]{1,0:T(8,128)(2,1)}, bf16[128,1024]{1,0:T(8,128)(2,1)S(1)}, u32[]{:S(2)}, u32[]{:S(2)}) collective-permute-start(bf16[128,1024]{1,0:T(8,128)(2,1)} %collective-permute-done.26), channel_id=1, source_target_pairs={{2,0},{3,1},{4,6},{5,7},{10,8},{11,9},{12,14},{13,15},{18,16},{19,... | collective-permute-start | bytes 786440 | tf_op jit(solution)/shard_map/ppermute | solution.py:49
  17.3 1.3 collective-permute-start.4
  19.5 1.2 collective-permute-start.23
  20.8 2.2 %collective-permute-start.29 = (bf16[128,1024]{1,0:T(8,128)(2,1)}, bf16[128,1024]{1,0:T(8,128)(2,1)S(1)}, u32[]{:S(2)}, u32[]{:S(2)}) collective-permute-start(bf16[128,1024]{1,0:T(8,128)(2,1)} %collective-permute-done.24.refs_2_), channel_id=1, source_target_pairs={{2,4},{3,5},{4,2},{5,3},{10,12},{11,13},{12,10},{13,11},{18,20},{1... | collective-permute-start | bytes 786440 | tf_op jit(solution)/shard_map/ppermute | solution.py:49
  23.0 1.0 broadcast_select_fusion.1.refs_4_
  24.1 1.3 collective-permute-start.25
  25.4 1.1 collective-permute-done.4
  26.5 2.2 %collective-permute-start.6 = (bf16[128,1024]{1,0:T(8,128)(2,1)S(1)}, bf16[128,1024]{1,0:T(8,128)(2,1)S(1)}, u32[]{:S(2)}, u32[]{:S(2)}) collective-permute-start(bf16[128,1024]{1,0:T(8,128)(2,1)S(1)} %collective-permute-done.1.refs_2_), channel_id=1, source_target_pairs={{2,4},{3,5},{4,2},{5,3},{10,12},{11,13},{12,10},{13,11},{18,20},{1... | collective-permute-start | bytes 786440 | tf_op jit(solution)/shard_map/ppermute | solution.py:49
  28.7 1.0 broadcast_select_fusion.3.refs_4_
  29.7 1.3 collective-permute-start.28
  31.0 1.5 collective-permute-start.30
  32.6 4.0 %collective-permute-done.6 = bf16[128,1024]{1,0:T(8,128)(2,1)S(1)} collective-permute-done((bf16[128,1024]{1,0:T(8,128)(2,1)S(1)}, bf16[128,1024]{1,0:T(8,128)(2,1)S(1)}, u32[]{:S(2)}, u32[]{:S(2)}) %collective-permute-start.6) | collective-permute-done | bytes 262176 | tf_op jit(solution)/shard_map/ppermute | solution.py:49
  36.7 1.5 collective-permute-start.7
  39.9 1.8 %collective-permute-start.12 = (bf16[2,2,2,128,128]{4,3,2,1,0:T(8,128)(2,1)}, bf16[2,2,2,128,128]{4,3,2,1,0:T(8,128)(2,1)S(1)}, u32[]{:S(2)}, u32[]{:S(2)}) collective-permute-start(bf16[2,2,2,128,128]{4,3,2,1,0:T(8,128)(2,1)} %pad_maximum_fusion.3), channel_id=1, source_target_pairs={{0,6},{1,7},{2,4},{3,5},{4,2},{5,3},{6,0},{7,1},{8,14},{9,15},{10,... | collective-permute-start | bytes 786440 | tf_op jit(solution)/shard_map/ppermute | solution.py:49
  42.0 3.5 %collective-permute-start.31 = (bf16[128,1024]{1,0:T(8,128)(2,1)S(1)}, bf16[128,1024]{1,0:T(8,128)(2,1)S(1)}, u32[]{:S(2)}, u32[]{:S(2)}) collective-permute-start(bf16[128,1024]{1,0:T(8,128)(2,1)S(1)} %broadcast_select_fusion.refs_6_), channel_id=1, source_target_pairs={{0,1},{1,0},{2,3},{3,2},{4,5},{5,4},{6,7},{7,6},{8,9},{9,8},{10,11... | collective-permute-start | bytes 786440 | tf_op jit(solution)/shard_map/ppermute | solution.py:49
  46.4 6.8 %collective-permute-done.10.refs_1_ = bf16[2,2,2,128,128]{4,3,2,1,0:T(8,128)(2,1)S(1)} collective-permute-done((bf16[2,2,2,128,128]{4,3,2,1,0:T(8,128)(2,1)S(1)}, bf16[2,2,2,128,128]{4,3,2,1,0:T(8,128)(2,1)S(1)}, u32[]{:S(2)}, u32[]{:S(2)}) %collective-permute-start.10) | collective-permute-done | bytes 262176 | tf_op jit(solution)/shard_map/ppermute | solution.py:49
  53.3 2.3 %collective-permute-start.2 = (bf16[128,1024]{1,0:T(8,128)(2,1)S(1)}, bf16[128,1024]{1,0:T(8,128)(2,1)S(1)}, u32[]{:S(2)}, u32[]{:S(2)}) collective-permute-start(bf16[128,1024]{1,0:T(8,128)(2,1)S(1)} %collective-permute-done.1.refs_2_), channel_id=1, source_target_pairs={{0,1},{1,0},{2,3},{3,2},{4,5},{5,4},{6,7},{7,6},{8,9},{9,8},{10,11... | collective-permute-start | bytes 786440 | tf_op jit(solution)/shard_map/ppermute | solution.py:49
  55.6 1.5 collective-permute-start.8
  57.1 10.0 %project.3 = (bf16[8,128,128]{2,1,0:T(8,128)(2,1)}, bf16[128,128]{1,0:T(8,128)(2,1)}, bf16[128,128]{1,0:T(8,128)(2,1)}) custom-call(s32[8]{0:T(128)} %broadcast_xor_fusion.source_ref, bf16[128,1024]{1,0:T(8,128)(2,1)} %copy-done.4, bf16[128,1024]{1,0:T(8,128)(2,1)} %copy-done.11, bf16[128,1024]{1,0:T(8,128)(2,1)} %collective-permute-done.24.refs_2_, ...), custom_call_target="tpu_custom_call" | custom-call | tf_op jit(solution)/shard_map/project/pallas_call | solution.py:155
  67.8 9.9 %attend_and_mix.3 = (bf16[128,1024]{1,0:T(8,128)(2,1)}, bf16[128,1024]{1,0:T(8,128)(2,1)}, bf16[128,1024]{1,0:T(8,128)(2,1)}, bf16[128,1024]{1,0:T(8,128)(2,1)},...) custom-call(s32[1]{0:T(128)} %bitcast.1.index_ref, ...), custom_call_target="tpu_custom_call" | custom-call | tf_op jit(solution)/shard_map/attend_and_mix/pallas_call | solution.py:250
  80.1 10.0 %project.2 = (bf16[8,128,128]{2,1,0:T(8,128)(2,1)}, bf16[128,128]{1,0:T(8,128)(2,1)}, bf16[128,128]{1,0:T(8,128)(2,1)}) custom-call(s32[8]{0:T(128)} %broadcast_xor_fusion.source_ref, bf16[128,1024]{1,0:T(8,128)(2,1)} %copy-done.3, bf16[128,1024]{1,0:T(8,128)(2,1)} %copy-done.14, bf16[128,1024]{1,0:T(8,128)(2,1)} %copy-done.10, ...), custom_call_target="tpu_custom_call" | custom-call | tf_op jit(solution)/shard_map/project/pallas_call | solution.py:155
  90.1 10.0 %attend_and_mix.2 = (bf16[128,1024]{1,0:T(8,128)(2,1)}, bf16[128,1024]{1,0:T(8,128)(2,1)}, bf16[128,1024]{1,0:T(8,128)(2,1)}, bf16[128,1024]{1,0:T(8,128)(2,1)},...) custom-call(s32[1]{0:T(128)} %bitcast.1.index_ref, ...), custom_call_target="tpu_custom_call" | custom-call | tf_op jit(solution)/shard_map/attend_and_mix/pallas_call | solution.py:250
  100.9 1.3 collective-permute-start.36
  103.1 2.5 %collective-permute-done.16 = bf16[128,1024]{1,0:T(8,128)(2,1)S(1)} collective-permute-done((bf16[128,1024]{1,0:T(8,128)(2,1)}, bf16[128,1024]{1,0:T(8,128)(2,1)S(1)}, u32[]{:S(2)}, u32[]{:S(2)}) %collective-permute-start.16) | collective-permute-done | bytes 262176 | tf_op jit(solution)/shard_map/ppermute | solution.py:49
  105.6 1.0 fusion.1
  106.7 1.3 collective-permute-start.17
  108.3 1.3 collective-permute-start.39
  112.1 2.1 %collective-permute-done.17 = bf16[128,1024]{1,0:T(8,128)(2,1)S(1)} collective-permute-done((bf16[128,1024]{1,0:T(8,128)(2,1)S(1)}, bf16[128,1024]{1,0:T(8,128)(2,1)S(1)}, u32[]{:S(2)}, u32[]{:S(2)}) %collective-permute-start.17) | collective-permute-done | bytes 262176 | tf_op jit(solution)/shard_map/ppermute | solution.py:49
  114.2 2.5 %collective-permute-start.37 = (bf16[128,1024]{1,0:T(8,128)(2,1)S(1)}, bf16[128,1024]{1,0:T(8,128)(2,1)S(1)}, u32[]{:S(2)}, u32[]{:S(2)}) collective-permute-start(bf16[128,1024]{1,0:T(8,128)(2,1)S(1)} %get-tuple-element.58), channel_id=1, source_target_pairs={{2,4},{3,5},{4,2},{5,3},{10,12},{11,13},{12,10},{13,11},{18,20},{1... | collective-permute-start | bytes 786440 | tf_op jit(solution)/shard_map/ppermute | solution.py:49
  116.7 1.1 add_convert_fusion.7
  117.8 2.8 %collective-permute-start.18 = (bf16[128,1024]{1,0:T(8,128)(2,1)S(1)}, bf16[128,1024]{1,0:T(8,128)(2,1)S(1)}, u32[]{:S(2)}, u32[]{:S(2)}) collective-permute-start(bf16[128,1024]{1,0:T(8,128)(2,1)S(1)} %get-tuple-element.62), channel_id=1, source_target_pairs={{2,4},{3,5},{4,2},{5,3},{10,12},{11,13},{12,10},{13,11},{18,20},{1... | collective-permute-start | bytes 786440 | tf_op jit(solution)/shard_map/ppermute | solution.py:49
  121.6 1.3 collective-permute-start.20
  123.0 3.5 %collective-permute-done.14 = bf16[128,1024]{1,0:T(8,128)(2,1)S(1)} collective-permute-done((bf16[128,1024]{1,0:T(8,128)(2,1)}, bf16[128,1024]{1,0:T(8,128)(2,1)S(1)}, u32[]{:S(2)}, u32[]{:S(2)}) %collective-permute-start.14) | collective-permute-done | bytes 262176 | tf_op jit(solution)/shard_map/ppermute | solution.py:49
  126.5 1.8 %collective-permute-start.38 = (bf16[128,1024]{1,0:T(8,128)(2,1)S(1)}, bf16[128,1024]{1,0:T(8,128)(2,1)S(1)}, u32[]{:S(2)}, u32[]{:S(2)}) collective-permute-start(bf16[128,1024]{1,0:T(8,128)(2,1)S(1)} %add_convert_fusion.2), channel_id=1, source_target_pairs={{0,2},{1,3},{2,0},{3,1},{4,6},{5,7},{6,4},{7,5},{8,10},{9,11},{10,... | collective-permute-start | bytes 786440 | tf_op jit(solution)/shard_map/ppermute | solution.py:49
  128.3 2.5 %collective-permute-start.40 = (bf16[128,1024]{1,0:T(8,128)(2,1)S(1)}, bf16[128,1024]{1,0:T(8,128)(2,1)S(1)}, u32[]{:S(2)}, u32[]{:S(2)}) collective-permute-start(bf16[128,1024]{1,0:T(8,128)(2,1)S(1)} %add_convert_fusion.1), channel_id=1, source_target_pairs={{2,4},{3,5},{4,2},{5,3},{10,12},{11,13},{12,10},{13,11},{18,20},{1... | collective-permute-start | bytes 786440 | tf_op jit(solution)/shard_map/ppermute | solution.py:49
  130.9 1.1 add_convert_fusion.6
  132.0 1.1 add_convert_fusion.5
  133.1 2.8 %collective-permute-start.21 = (bf16[128,1024]{1,0:T(8,128)(2,1)S(1)}, bf16[128,1024]{1,0:T(8,128)(2,1)S(1)}, u32[]{:S(2)}, u32[]{:S(2)}) collective-permute-start(bf16[128,1024]{1,0:T(8,128)(2,1)S(1)} %add_convert_fusion.5), channel_id=1, source_target_pairs={{2,4},{3,5},{4,2},{5,3},{10,12},{11,13},{12,10},{13,11},{18,20},{1... | collective-permute-start | bytes 786440 | tf_op jit(solution)/shard_map/ppermute | solution.py:49
  135.9 1.4 collective-permute-done.38
  137.5 18.1 %collective-permute-start.41 = (bf16[128,1024]{1,0:T(8,128)(2,1)S(1)}, bf16[128,1024]{1,0:T(8,128)(2,1)S(1)}, u32[]{:S(2)}, u32[]{:S(2)}) collective-permute-start(bf16[128,1024]{1,0:T(8,128)(2,1)S(1)} %add_convert_fusion), channel_id=1, source_target_pairs={{0,8},{8,0},{1,9},{9,1},{2,10},{10,2},{3,11},{11,3},{4,12},{12,4},... | collective-permute-start | bytes 786440 | tf_op jit(solution)/shard_map/ppermute | solution.py:469
  155.6 1.1 add_convert_fusion.4
  156.7 5.0 %collective-permute-start.22 = (bf16[128,1024]{1,0:T(8,128)(2,1)S(1)}, bf16[128,1024]{1,0:T(8,128)(2,1)S(1)}, u32[]{:S(2)}, u32[]{:S(2)}) collective-permute-start(bf16[128,1024]{1,0:T(8,128)(2,1)S(1)} %add_convert_fusion.4), channel_id=1, source_target_pairs={{0,8},{8,0},{1,9},{9,1},{2,10},{10,2},{3,11},{11,3},{4,12},{12,4},... | collective-permute-start | bytes 786440 | tf_op jit(solution)/shard_map/ppermute | solution.py:469
  162.9 7.7 %select_bitcast_fusion.2 = (bf16[1,128,1024]{2,1,0:T(8,128)(2,1)S(1)}, bf16[1,128,1024]{2,1,0:T(8,128)(2,1)S(1)}, bf16[1,128,1024]{2,1,0:T(8,128)(2,1)S(1)}) fusion(bf16[128,1024]{1,0:T(8,128)(2,1)S(1)} %collective-permute-done.22, bf16[128,1024]{1,0:T(8,128)(2,1)S(1)} %collective-permute-done.41, bf16[128,1024]{1,0:T(8,128)(2,1)S(1)} %add_convert_fusion.4, ...), kind=kLoop, calls=%fused_computation.24 | loop fusion | flops 1572864 | bytes 1835020 | tf_op jit(solution)/shard_map/stack | solution.py:472
  170.6 1.0 maximum_bitcast_fusion
  (132 shorter events, 19.4 us)
Async XLA Ops:
  1.1 56.0 %copy-start.4 = (bf16[128,1024]{1,0:T(8,128)(2,1)}, bf16[128,1024]{1,0:T(8,128)(2,1)S(1)}, u32[]{:S(2)}) copy-start(bf16[128,1024]{1,0:T(8,128)(2,1)S(1)} %get-tuple-element.60.refs_0_) | copy-start | bytes 786436
  1.1 66.0 %copy-start.3 = (bf16[128,1024]{1,0:T(8,128)(2,1)}, bf16[128,1024]{1,0:T(8,128)(2,1)S(1)}, u32[]{:S(2)}) copy-start(bf16[128,1024]{1,0:T(8,128)(2,1)S(1)} %get-tuple-element.61.refs_0_) | copy-start | bytes 786436
  1.1 18.4 %collective-permute-start.24 = (bf16[128,1024]{1,0:T(8,128)(2,1)S(1)}, bf16[128,1024]{1,0:T(8,128)(2,1)}, u32[]{:S(2)}, u32[]{:S(2)}) collective-permute-start(bf16[128,1024]{1,0:T(8,128)(2,1)S(1)} %get-tuple-element.60.refs_0_), channel_id=1, source_target_pairs={{0,2},{1,3},{2,0},{3,1},{4,6},{5,7},{6,4},{7,5},{8,10},{9,11},{10,... | collective-permute-start | bytes 786440 | tf_op jit(solution)/shard_map/ppermute | solution.py:49
  1.3 12.6 %collective-permute-start.26 = (bf16[128,1024]{1,0:T(8,128)(2,1)S(1)}, bf16[128,1024]{1,0:T(8,128)(2,1)}, u32[]{:S(2)}, u32[]{:S(2)}) collective-permute-start(bf16[128,1024]{1,0:T(8,128)(2,1)S(1)} %get-tuple-element.60.refs_0_), channel_id=1, source_target_pairs={{2,4},{3,5},{4,2},{5,3},{10,12},{11,13},{12,10},{13,11},{18,20},{1... | collective-permute-start | bytes 786440 | tf_op jit(solution)/shard_map/ppermute | solution.py:49
  5.7 18.4 %collective-permute-start.1 = (bf16[128,1024]{1,0:T(8,128)(2,1)S(1)}, bf16[128,1024]{1,0:T(8,128)(2,1)S(1)}, u32[]{:S(2)}, u32[]{:S(2)}) collective-permute-start(bf16[128,1024]{1,0:T(8,128)(2,1)S(1)} %get-tuple-element.61.refs_0_), channel_id=1, source_target_pairs={{0,2},{1,3},{2,0},{3,1},{4,6},{5,7},{6,4},{7,5},{8,10},{9,11},{10,... | collective-permute-start | bytes 786440 | tf_op jit(solution)/shard_map/ppermute | solution.py:49
  5.7 11.6 %collective-permute-start.3 = (bf16[128,1024]{1,0:T(8,128)(2,1)S(1)}, bf16[128,1024]{1,0:T(8,128)(2,1)}, u32[]{:S(2)}, u32[]{:S(2)}) collective-permute-start(bf16[128,1024]{1,0:T(8,128)(2,1)S(1)} %get-tuple-element.61.refs_0_), channel_id=1, source_target_pairs={{2,4},{3,5},{4,2},{5,3},{10,12},{11,13},{12,10},{13,11},{18,20},{1... | collective-permute-start | bytes 786440 | tf_op jit(solution)/shard_map/ppermute | solution.py:49
  10.5 20.4 %collective-permute-start.9 = (bf16[4,2,2,128,128]{4,3,2,1,0:T(8,128)(2,1)}, bf16[4,2,2,128,128]{4,3,2,1,0:T(8,128)(2,1)S(1)}, u32[]{:S(2)}, u32[]{:S(2)}) collective-permute-start(bf16[4,2,2,128,128]{4,3,2,1,0:T(8,128)(2,1)} %dynamic-slice_bitcast_fusion), channel_id=1, source_target_pairs={{0,1},{1,0},{2,3},{3,2},{4,5},{5,4},{6,7},{7,6},{8,9},{9,8},{10,11... | collective-permute-start | bytes 1572872 | tf_op jit(solution)/shard_map/ppermute | solution.py:49
  13.9 6.9 %collective-permute-start.27 = (bf16[128,1024]{1,0:T(8,128)(2,1)}, bf16[128,1024]{1,0:T(8,128)(2,1)S(1)}, u32[]{:S(2)}, u32[]{:S(2)}) collective-permute-start(bf16[128,1024]{1,0:T(8,128)(2,1)} %collective-permute-done.26), channel_id=1, source_target_pairs={{2,0},{3,1},{4,6},{5,7},{10,8},{11,9},{12,14},{13,15},{18,16},{19,... | collective-permute-start | bytes 786440 | tf_op jit(solution)/shard_map/ppermute | solution.py:49
  17.3 9.1 %collective-permute-start.4 = (bf16[128,1024]{1,0:T(8,128)(2,1)}, bf16[128,1024]{1,0:T(8,128)(2,1)S(1)}, u32[]{:S(2)}, u32[]{:S(2)}) collective-permute-start(bf16[128,1024]{1,0:T(8,128)(2,1)} %collective-permute-done.3), channel_id=1, source_target_pairs={{2,0},{3,1},{4,6},{5,7},{10,8},{11,9},{12,14},{13,15},{18,16},{19,... | collective-permute-start | bytes 786440 | tf_op jit(solution)/shard_map/ppermute | solution.py:49
  19.5 19.5 %collective-permute-start.23 = (bf16[128,1024]{1,0:T(8,128)(2,1)S(1)}, bf16[128,1024]{1,0:T(8,128)(2,1)S(1)}, u32[]{:S(2)}, u32[]{:S(2)}) collective-permute-start(bf16[128,1024]{1,0:T(8,128)(2,1)S(1)} %get-tuple-element.60.refs_0_), channel_id=1, source_target_pairs={{0,1},{1,0},{2,3},{3,2},{4,5},{5,4},{6,7},{7,6},{8,9},{9,8},{10,11... | collective-permute-start | bytes 786440 | tf_op jit(solution)/shard_map/ppermute | solution.py:49
  20.8 8.8 %collective-permute-start.29 = (bf16[128,1024]{1,0:T(8,128)(2,1)}, bf16[128,1024]{1,0:T(8,128)(2,1)S(1)}, u32[]{:S(2)}, u32[]{:S(2)}) collective-permute-start(bf16[128,1024]{1,0:T(8,128)(2,1)} %collective-permute-done.24.refs_2_), channel_id=1, source_target_pairs={{2,4},{3,5},{4,2},{5,3},{10,12},{11,13},{12,10},{13,11},{18,20},{1... | collective-permute-start | bytes 786440 | tf_op jit(solution)/shard_map/ppermute | solution.py:49
  24.0 33.1 %copy-start.6 = (bf16[128,1024]{1,0:T(8,128)(2,1)}, bf16[128,1024]{1,0:T(8,128)(2,1)S(1)}, u32[]{:S(2)}) copy-start(bf16[128,1024]{1,0:T(8,128)(2,1)S(1)} %broadcast_select_fusion.1.refs_4_) | copy-start | bytes 786436
  24.0 53.7 %copy-start.10 = (bf16[128,1024]{1,0:T(8,128)(2,1)}, bf16[128,1024]{1,0:T(8,128)(2,1)S(1)}, u32[]{:S(2)}) copy-start(bf16[128,1024]{1,0:T(8,128)(2,1)S(1)} %collective-permute-done.1.refs_2_) | copy-start | bytes 786436
  24.1 15.9 %collective-permute-start.25 = (bf16[128,1024]{1,0:T(8,128)(2,1)}, bf16[128,1024]{1,0:T(8,128)(2,1)S(1)}, u32[]{:S(2)}, u32[]{:S(2)}) collective-permute-start(bf16[128,1024]{1,0:T(8,128)(2,1)} %collective-permute-done.24.refs_2_), channel_id=1, source_target_pairs={{0,1},{1,0},{2,3},{3,2},{4,5},{5,4},{6,7},{7,6},{8,9},{9,8},{10,11... | collective-permute-start | bytes 786440 | tf_op jit(solution)/shard_map/ppermute | solution.py:49
  26.5 10.2 %collective-permute-start.6 = (bf16[128,1024]{1,0:T(8,128)(2,1)S(1)}, bf16[128,1024]{1,0:T(8,128)(2,1)S(1)}, u32[]{:S(2)}, u32[]{:S(2)}) collective-permute-start(bf16[128,1024]{1,0:T(8,128)(2,1)S(1)} %collective-permute-done.1.refs_2_), channel_id=1, source_target_pairs={{2,4},{3,5},{4,2},{5,3},{10,12},{11,13},{12,10},{13,11},{18,20},{1... | collective-permute-start | bytes 786440 | tf_op jit(solution)/shard_map/ppermute | solution.py:49
  29.7 48.1 %copy-start.5 = (bf16[128,1024]{1,0:T(8,128)(2,1)}, bf16[128,1024]{1,0:T(8,128)(2,1)S(1)}, u32[]{:S(2)}) copy-start(bf16[128,1024]{1,0:T(8,128)(2,1)S(1)} %broadcast_select_fusion.3.refs_4_) | copy-start | bytes 786436
  29.7 16.7 %collective-permute-start.28 = (bf16[128,1024]{1,0:T(8,128)(2,1)S(1)}, bf16[128,1024]{1,0:T(8,128)(2,1)S(1)}, u32[]{:S(2)}, u32[]{:S(2)}) collective-permute-start(bf16[128,1024]{1,0:T(8,128)(2,1)S(1)} %broadcast_select_fusion.1.refs_4_), channel_id=1, source_target_pairs={{0,1},{1,0},{2,3},{3,2},{4,5},{5,4},{6,7},{7,6},{8,9},{9,8},{10,11... | collective-permute-start | bytes 786440 | tf_op jit(solution)/shard_map/ppermute | solution.py:49
  31.0 7.9 %collective-permute-start.30 = (bf16[128,1024]{1,0:T(8,128)(2,1)S(1)}, bf16[128,1024]{1,0:T(8,128)(2,1)S(1)}, u32[]{:S(2)}, u32[]{:S(2)}) collective-permute-start(bf16[128,1024]{1,0:T(8,128)(2,1)S(1)} %collective-permute-done.29), channel_id=1, source_target_pairs={{2,0},{3,1},{4,6},{5,7},{10,8},{11,9},{12,14},{13,15},{18,16},{19,... | collective-permute-start | bytes 786440 | tf_op jit(solution)/shard_map/ppermute | solution.py:49
  36.7 5.4 %collective-permute-start.7 = (bf16[128,1024]{1,0:T(8,128)(2,1)S(1)}, bf16[128,1024]{1,0:T(8,128)(2,1)S(1)}, u32[]{:S(2)}, u32[]{:S(2)}) collective-permute-start(bf16[128,1024]{1,0:T(8,128)(2,1)S(1)} %collective-permute-done.6), channel_id=1, source_target_pairs={{2,0},{3,1},{4,6},{5,7},{10,8},{11,9},{12,14},{13,15},{18,16},{19,... | collective-permute-start | bytes 786440 | tf_op jit(solution)/shard_map/ppermute | solution.py:49
  38.9 14.4 %collective-permute-start.10 = (bf16[2,2,2,128,128]{4,3,2,1,0:T(8,128)(2,1)S(1)}, bf16[2,2,2,128,128]{4,3,2,1,0:T(8,128)(2,1)S(1)}, u32[]{:S(2)}, u32[]{:S(2)}) collective-permute-start(bf16[2,2,2,128,128]{4,3,2,1,0:T(8,128)(2,1)S(1)} %pad_maximum_fusion.1), channel_id=1, source_target_pairs={{0,2},{1,3},{2,0},{3,1},{4,6},{5,7},{6,4},{7,5},{8,10},{9,11},{10,... | collective-permute-start | bytes 786440 | tf_op jit(solution)/shard_map/ppermute | solution.py:49
  39.0 16.6 %collective-permute-start.11 = (bf16[2,2,2,128,128]{4,3,2,1,0:T(8,128)(2,1)S(1)}, bf16[2,2,2,128,128]{4,3,2,1,0:T(8,128)(2,1)S(1)}, u32[]{:S(2)}, u32[]{:S(2)}) collective-permute-start(bf16[2,2,2,128,128]{4,3,2,1,0:T(8,128)(2,1)S(1)} %pad_maximum_fusion.2), channel_id=1, source_target_pairs={{0,4},{1,5},{2,6},{3,7},{4,0},{5,1},{6,2},{7,3},{8,12},{9,13},{10,... | collective-permute-start | bytes 786440 | tf_op jit(solution)/shard_map/ppermute | solution.py:49
  39.9 27.2 %collective-permute-start.12 = (bf16[2,2,2,128,128]{4,3,2,1,0:T(8,128)(2,1)}, bf16[2,2,2,128,128]{4,3,2,1,0:T(8,128)(2,1)S(1)}, u32[]{:S(2)}, u32[]{:S(2)}) collective-permute-start(bf16[2,2,2,128,128]{4,3,2,1,0:T(8,128)(2,1)} %pad_maximum_fusion.3), channel_id=1, source_target_pairs={{0,6},{1,7},{2,4},{3,5},{4,2},{5,3},{6,0},{7,1},{8,14},{9,15},{10,... | collective-permute-start | bytes 786440 | tf_op jit(solution)/shard_map/ppermute | solution.py:49
  42.0 13.6 %collective-permute-start.31 = (bf16[128,1024]{1,0:T(8,128)(2,1)S(1)}, bf16[128,1024]{1,0:T(8,128)(2,1)S(1)}, u32[]{:S(2)}, u32[]{:S(2)}) collective-permute-start(bf16[128,1024]{1,0:T(8,128)(2,1)S(1)} %broadcast_select_fusion.refs_6_), channel_id=1, source_target_pairs={{0,1},{1,0},{2,3},{3,2},{4,5},{5,4},{6,7},{7,6},{8,9},{9,8},{10,11... | collective-permute-start | bytes 786440 | tf_op jit(solution)/shard_map/ppermute | solution.py:49
  46.4 32.1 %collective-permute-start = (bf16[128,1024]{1,0:T(8,128)(2,1)S(1)}, bf16[128,1024]{1,0:T(8,128)(2,1)S(1)}, u32[]{:S(2)}, u32[]{:S(2)}) collective-permute-start(bf16[128,1024]{1,0:T(8,128)(2,1)S(1)} %get-tuple-element.61.refs_0_), channel_id=1, source_target_pairs={{0,1},{1,0},{2,3},{3,2},{4,5},{5,4},{6,7},{7,6},{8,9},{9,8},{10,11... | collective-permute-start | bytes 786440 | tf_op jit(solution)/shard_map/ppermute | solution.py:49
  53.3 26.0 %collective-permute-start.2 = (bf16[128,1024]{1,0:T(8,128)(2,1)S(1)}, bf16[128,1024]{1,0:T(8,128)(2,1)S(1)}, u32[]{:S(2)}, u32[]{:S(2)}) collective-permute-start(bf16[128,1024]{1,0:T(8,128)(2,1)S(1)} %collective-permute-done.1.refs_2_), channel_id=1, source_target_pairs={{0,1},{1,0},{2,3},{3,2},{4,5},{5,4},{6,7},{7,6},{8,9},{9,8},{10,11... | collective-permute-start | bytes 786440 | tf_op jit(solution)/shard_map/ppermute | solution.py:49
  55.5 23.8 %collective-permute-start.5 = (bf16[128,1024]{1,0:T(8,128)(2,1)S(1)}, bf16[128,1024]{1,0:T(8,128)(2,1)}, u32[]{:S(2)}, u32[]{:S(2)}) collective-permute-start(bf16[128,1024]{1,0:T(8,128)(2,1)S(1)} %broadcast_select_fusion.3.refs_4_), channel_id=1, source_target_pairs={{0,1},{1,0},{2,3},{3,2},{4,5},{5,4},{6,7},{7,6},{8,9},{9,8},{10,11... | collective-permute-start | bytes 786440 | tf_op jit(solution)/shard_map/ppermute | solution.py:49
  55.6 23.7 %collective-permute-start.8 = (bf16[128,1024]{1,0:T(8,128)(2,1)S(1)}, bf16[128,1024]{1,0:T(8,128)(2,1)}, u32[]{:S(2)}, u32[]{:S(2)}) collective-permute-start(bf16[128,1024]{1,0:T(8,128)(2,1)S(1)} %broadcast_select_fusion.2.refs_6_), channel_id=1, source_target_pairs={{0,1},{1,0},{2,3},{3,2},{4,5},{5,4},{6,7},{7,6},{8,9},{9,8},{10,11... | collective-permute-start | bytes 786440 | tf_op jit(solution)/shard_map/ppermute | solution.py:49
  77.8 23.1 %collective-permute-start.35 = (bf16[128,1024]{1,0:T(8,128)(2,1)}, bf16[128,1024]{1,0:T(8,128)(2,1)S(1)}, u32[]{:S(2)}, u32[]{:S(2)}) collective-permute-start(bf16[128,1024]{1,0:T(8,128)(2,1)} %get-tuple-element.48), channel_id=1, source_target_pairs={{0,1},{1,0},{2,3},{3,2},{4,5},{5,4},{6,7},{7,6},{8,9},{9,8},{10,11... | collective-permute-start | bytes 786440 | tf_op jit(solution)/shard_map/ppermute | solution.py:49
  78.5 29.5 %collective-permute-start.34 = (bf16[128,1024]{1,0:T(8,128)(2,1)}, bf16[128,1024]{1,0:T(8,128)(2,1)S(1)}, u32[]{:S(2)}, u32[]{:S(2)}) collective-permute-start(bf16[128,1024]{1,0:T(8,128)(2,1)} %get-tuple-element.46), channel_id=1, source_target_pairs={{0,1},{1,0},{2,3},{3,2},{4,5},{5,4},{6,7},{7,6},{8,9},{9,8},{10,11... | collective-permute-start | bytes 786440 | tf_op jit(solution)/shard_map/ppermute | solution.py:49
  90.1 47.2 %copy-start.17 = (bf16[128,1024]{1,0:T(8,128)(2,1)S(1)}, bf16[128,1024]{1,0:T(8,128)(2,1)}, u32[]{:S(2)}) copy-start(bf16[128,1024]{1,0:T(8,128)(2,1)} %get-tuple-element.41) | copy-start | bytes 786436
  100.1 5.5 %collective-permute-start.16 = (bf16[128,1024]{1,0:T(8,128)(2,1)}, bf16[128,1024]{1,0:T(8,128)(2,1)S(1)}, u32[]{:S(2)}, u32[]{:S(2)}) collective-permute-start(bf16[128,1024]{1,0:T(8,128)(2,1)} %get-tuple-element.37), channel_id=1, source_target_pairs={{0,1},{1,0},{2,3},{3,2},{4,5},{5,4},{6,7},{7,6},{8,9},{9,8},{10,11... | collective-permute-start | bytes 786440 | tf_op jit(solution)/shard_map/ppermute | solution.py:49
  100.9 7.2 %collective-permute-start.36 = (bf16[128,1024]{1,0:T(8,128)(2,1)S(1)}, bf16[128,1024]{1,0:T(8,128)(2,1)S(1)}, u32[]{:S(2)}, u32[]{:S(2)}) collective-permute-start(bf16[128,1024]{1,0:T(8,128)(2,1)S(1)} %fusion.3), channel_id=1, source_target_pairs={{0,2},{1,3},{6,4},{7,5},{8,10},{9,11},{14,12},{15,13},{16,18},{17,... | collective-permute-start | bytes 786440 | tf_op jit(solution)/shard_map/ppermute | solution.py:49
  102.2 9.0 %collective-permute-start.15 = (bf16[128,1024]{1,0:T(8,128)(2,1)}, bf16[128,1024]{1,0:T(8,128)(2,1)S(1)}, u32[]{:S(2)}, u32[]{:S(2)}) collective-permute-start(bf16[128,1024]{1,0:T(8,128)(2,1)} %get-tuple-element.35), channel_id=1, source_target_pairs={{0,1},{1,0},{2,3},{3,2},{4,5},{5,4},{6,7},{7,6},{8,9},{9,8},{10,11... | collective-permute-start | bytes 786440 | tf_op jit(solution)/shard_map/ppermute | solution.py:49
  106.7 7.5 %collective-permute-start.17 = (bf16[128,1024]{1,0:T(8,128)(2,1)S(1)}, bf16[128,1024]{1,0:T(8,128)(2,1)S(1)}, u32[]{:S(2)}, u32[]{:S(2)}) collective-permute-start(bf16[128,1024]{1,0:T(8,128)(2,1)S(1)} %fusion.1), channel_id=1, source_target_pairs={{0,2},{1,3},{6,4},{7,5},{8,10},{9,11},{14,12},{15,13},{16,18},{17,... | collective-permute-start | bytes 786440 | tf_op jit(solution)/shard_map/ppermute | solution.py:49
  108.3 9.5 %collective-permute-start.39 = (bf16[128,1024]{1,0:T(8,128)(2,1)S(1)}, bf16[128,1024]{1,0:T(8,128)(2,1)S(1)}, u32[]{:S(2)}, u32[]{:S(2)}) collective-permute-start(bf16[128,1024]{1,0:T(8,128)(2,1)S(1)} %get-tuple-element.59), channel_id=1, source_target_pairs={{0,2},{1,3},{6,4},{7,5},{8,10},{9,11},{14,12},{15,13},{16,18},{17,... | collective-permute-start | bytes 786440 | tf_op jit(solution)/shard_map/ppermute | solution.py:49
  109.7 11.0 %collective-permute-start.33 = (bf16[128,1024]{1,0:T(8,128)(2,1)S(1)}, bf16[128,1024]{1,0:T(8,128)(2,1)S(1)}, u32[]{:S(2)}, u32[]{:S(2)}) collective-permute-start(bf16[128,1024]{1,0:T(8,128)(2,1)S(1)} %copy-done.22), channel_id=1, source_target_pairs={{0,1},{1,0},{2,3},{3,2},{4,5},{5,4},{6,7},{7,6},{8,9},{9,8},{10,11... | collective-permute-start | bytes 786440 | tf_op jit(solution)/shard_map/ppermute | solution.py:49
  110.6 22.5 %collective-permute-start.32 = (bf16[128,1024]{1,0:T(8,128)(2,1)S(1)}, bf16[128,1024]{1,0:T(8,128)(2,1)S(1)}, u32[]{:S(2)}, u32[]{:S(2)}) collective-permute-start(bf16[128,1024]{1,0:T(8,128)(2,1)S(1)} %copy-done.21), channel_id=1, source_target_pairs={{0,1},{1,0},{2,3},{3,2},{4,5},{5,4},{6,7},{7,6},{8,9},{9,8},{10,11... | collective-permute-start | bytes 786440 | tf_op jit(solution)/shard_map/ppermute | solution.py:49
  111.3 15.3 %collective-permute-start.14 = (bf16[128,1024]{1,0:T(8,128)(2,1)}, bf16[128,1024]{1,0:T(8,128)(2,1)S(1)}, u32[]{:S(2)}, u32[]{:S(2)}) collective-permute-start(bf16[128,1024]{1,0:T(8,128)(2,1)} %get-tuple-element.33), channel_id=1, source_target_pairs={{0,1},{1,0},{2,3},{3,2},{4,5},{5,4},{6,7},{7,6},{8,9},{9,8},{10,11... | collective-permute-start | bytes 786440 | tf_op jit(solution)/shard_map/ppermute | solution.py:49
  114.2 7.4 %collective-permute-start.37 = (bf16[128,1024]{1,0:T(8,128)(2,1)S(1)}, bf16[128,1024]{1,0:T(8,128)(2,1)S(1)}, u32[]{:S(2)}, u32[]{:S(2)}) collective-permute-start(bf16[128,1024]{1,0:T(8,128)(2,1)S(1)} %get-tuple-element.58), channel_id=1, source_target_pairs={{2,4},{3,5},{4,2},{5,3},{10,12},{11,13},{12,10},{13,11},{18,20},{1... | collective-permute-start | bytes 786440 | tf_op jit(solution)/shard_map/ppermute | solution.py:49
  117.8 10.5 %collective-permute-start.18 = (bf16[128,1024]{1,0:T(8,128)(2,1)S(1)}, bf16[128,1024]{1,0:T(8,128)(2,1)S(1)}, u32[]{:S(2)}, u32[]{:S(2)}) collective-permute-start(bf16[128,1024]{1,0:T(8,128)(2,1)S(1)} %get-tuple-element.62), channel_id=1, source_target_pairs={{2,4},{3,5},{4,2},{5,3},{10,12},{11,13},{12,10},{13,11},{18,20},{1... | collective-permute-start | bytes 786440 | tf_op jit(solution)/shard_map/ppermute | solution.py:49
  120.7 34.9 %collective-permute-start.13 = (bf16[128,1024]{1,0:T(8,128)(2,1)}, bf16[128,1024]{1,0:T(8,128)(2,1)S(1)}, u32[]{:S(2)}, u32[]{:S(2)}) collective-permute-start(bf16[128,1024]{1,0:T(8,128)(2,1)} %get-tuple-element.31), channel_id=1, source_target_pairs={{0,1},{1,0},{2,3},{3,2},{4,5},{5,4},{6,7},{7,6},{8,9},{9,8},{10,11... | collective-permute-start | bytes 786440 | tf_op jit(solution)/shard_map/ppermute | solution.py:49
  121.6 10.4 %collective-permute-start.20 = (bf16[128,1024]{1,0:T(8,128)(2,1)S(1)}, bf16[128,1024]{1,0:T(8,128)(2,1)S(1)}, u32[]{:S(2)}, u32[]{:S(2)}) collective-permute-start(bf16[128,1024]{1,0:T(8,128)(2,1)S(1)} %get-tuple-element.63), channel_id=1, source_target_pairs={{0,2},{1,3},{6,4},{7,5},{8,10},{9,11},{14,12},{15,13},{16,18},{17,... | collective-permute-start | bytes 786440 | tf_op jit(solution)/shard_map/ppermute | solution.py:49
  126.5 10.8 %collective-permute-start.38 = (bf16[128,1024]{1,0:T(8,128)(2,1)S(1)}, bf16[128,1024]{1,0:T(8,128)(2,1)S(1)}, u32[]{:S(2)}, u32[]{:S(2)}) collective-permute-start(bf16[128,1024]{1,0:T(8,128)(2,1)S(1)} %add_convert_fusion.2), channel_id=1, source_target_pairs={{0,2},{1,3},{2,0},{3,1},{4,6},{5,7},{6,4},{7,5},{8,10},{9,11},{10,... | collective-permute-start | bytes 786440 | tf_op jit(solution)/shard_map/ppermute | solution.py:49
  128.3 9.0 %collective-permute-start.40 = (bf16[128,1024]{1,0:T(8,128)(2,1)S(1)}, bf16[128,1024]{1,0:T(8,128)(2,1)S(1)}, u32[]{:S(2)}, u32[]{:S(2)}) collective-permute-start(bf16[128,1024]{1,0:T(8,128)(2,1)S(1)} %add_convert_fusion.1), channel_id=1, source_target_pairs={{2,4},{3,5},{4,2},{5,3},{10,12},{11,13},{12,10},{13,11},{18,20},{1... | collective-permute-start | bytes 786440 | tf_op jit(solution)/shard_map/ppermute | solution.py:49
  132.0 23.7 %collective-permute-start.19 = (bf16[128,1024]{1,0:T(8,128)(2,1)S(1)}, bf16[128,1024]{1,0:T(8,128)(2,1)S(1)}, u32[]{:S(2)}, u32[]{:S(2)}) collective-permute-start(bf16[128,1024]{1,0:T(8,128)(2,1)S(1)} %add_convert_fusion.6), channel_id=1, source_target_pairs={{0,2},{1,3},{2,0},{3,1},{4,6},{5,7},{6,4},{7,5},{8,10},{9,11},{10,... | collective-permute-start | bytes 786440 | tf_op jit(solution)/shard_map/ppermute | solution.py:49
  133.1 22.5 %collective-permute-start.21 = (bf16[128,1024]{1,0:T(8,128)(2,1)S(1)}, bf16[128,1024]{1,0:T(8,128)(2,1)S(1)}, u32[]{:S(2)}, u32[]{:S(2)}) collective-permute-start(bf16[128,1024]{1,0:T(8,128)(2,1)S(1)} %add_convert_fusion.5), channel_id=1, source_target_pairs={{2,4},{3,5},{4,2},{5,3},{10,12},{11,13},{12,10},{13,11},{18,20},{1... | collective-permute-start | bytes 786440 | tf_op jit(solution)/shard_map/ppermute | solution.py:49
  137.5 25.0 %collective-permute-start.41 = (bf16[128,1024]{1,0:T(8,128)(2,1)S(1)}, bf16[128,1024]{1,0:T(8,128)(2,1)S(1)}, u32[]{:S(2)}, u32[]{:S(2)}) collective-permute-start(bf16[128,1024]{1,0:T(8,128)(2,1)S(1)} %add_convert_fusion), channel_id=1, source_target_pairs={{0,8},{8,0},{1,9},{9,1},{2,10},{10,2},{3,11},{11,3},{4,12},{12,4},... | collective-permute-start | bytes 786440 | tf_op jit(solution)/shard_map/ppermute | solution.py:469
  156.7 6.2 %collective-permute-start.22 = (bf16[128,1024]{1,0:T(8,128)(2,1)S(1)}, bf16[128,1024]{1,0:T(8,128)(2,1)S(1)}, u32[]{:S(2)}, u32[]{:S(2)}) collective-permute-start(bf16[128,1024]{1,0:T(8,128)(2,1)S(1)} %add_convert_fusion.4), channel_id=1, source_target_pairs={{0,8},{8,0},{1,9},{9,1},{2,10},{10,2},{3,11},{11,3},{4,12},{12,4},... | collective-permute-start | bytes 786440 | tf_op jit(solution)/shard_map/ppermute | solution.py:469
  (17 other events, 287.4 us)
